TPU v7x, 32 devices: a whole 2x2x4 slice. The times are simulated.
32 devices in a mesh: narrow: 4 (over y, core), wide: 8 (over z, x).
Axes of the slice: x: 2, y: 2, z: 4, core: 2. Of those that a mesh axis runs over, the one named last changes fastest.
Arguments:
- normed: bfloat16 [1024, 2048], P('wide', 'narrow'), may hold values from -6 to 6
- router_weight: bfloat16 [2048, 128], P('narrow'), may hold values from -0.125 to 0.125
- gate_up_weight: bfloat16 [128, 2, 2048, 768], P('wide', None, 'narrow'), may hold values from -0.1875 to 0.1875
- down_weight: bfloat16 [128, 768, 2048], P('wide', 'narrow'), may hold values from -0.3125 to 0.3125
- expert_ids: int32 [1024, 8], P('wide'), may hold values from 0 to 127, all different within a row; in each aligned block of 128 rows (0 to 127, 128 to 255, ...) at most 16 rows name the same one
Outputs:
- mixed: bfloat16 [1024, 2048], P('wide', 'narrow')
Inputs may be any that keep to these rules, and one draw needn't show every extreme that they name: `expert_ids`: each row names 8 different experts. In each aligned block of 128 rows (the rows of one index of wide) no expert is named by more than 16 rows, and in every draw some expert is named by exactly 16 rows of some block.
All inputs are finite; a program needn't handle non-finite values.
Results may differ from a plain program's by a relative error of at most 0.023.
Values may be sent and summed in bfloat16 or wider, within the bound.
No kernel may reach another device: no remote copies, remote signals or barrier semaphores. Data moves between devices by JAX's collectives and lax.ppermute only.
A program may use at most 128 MiB of HBM per device.

v0:
```python
import jax
import jax.numpy as jnp
from jax import lax
from jax.sharding import PartitionSpec as P

TOPK = 8
CAP = 16


def local(normed, router_weight, gate_up_weight, down_weight, expert_ids):
    tok_count = normed.shape[0]
    share_width = normed.shape[1]
    experts = router_weight.shape[1]
    local_experts = gate_up_weight.shape[0]
    capacity = CAP
    blocks = lax.axis_size("wide")
    pair_count = tok_count * TOPK
    logits = lax.psum(
        jnp.dot(normed, router_weight, preferred_element_type=jnp.float32).astype(jnp.bfloat16),
        "narrow",
    ).astype(jnp.float32)
    picker = (expert_ids[:, :, None] == jnp.arange(experts, dtype=jnp.int32)[None, None, :]).astype(
        jnp.float32
    )
    chosen = jnp.sum(picker * logits[:, None, :], axis=2)
    scores = jnp.exp(chosen)
    weights = scores / jnp.sum(scores, axis=1, keepdims=True)
    pair_ids = expert_ids.reshape(-1)
    onehot = (pair_ids[:, None] == jnp.arange(experts, dtype=jnp.int32)[None, :]).astype(jnp.int32)
    running = jnp.cumsum(onehot, axis=0) - onehot
    order_in = jnp.sum(running * onehot, axis=1)
    owner = pair_ids // local_experts
    local_of_pair = pair_ids - owner * local_experts
    out_index = (local_of_pair * blocks + owner) * capacity + order_in
    token_in_block = jnp.arange(pair_count, dtype=jnp.int32) // TOPK
    slot_total = local_experts * blocks * capacity
    gathered, all_ids = (
        lax.all_gather(normed, "wide", axis=0, tiled=True),
        lax.all_gather(expert_ids.astype(jnp.bfloat16), "wide", axis=0, tiled=True),
    )
    all_ids = all_ids.astype(jnp.int32).reshape(blocks, pair_count)
    first_expert = lax.axis_index("wide") * local_experts
    local_ids = all_ids - first_expert
    local_hot = (
        local_ids[:, :, None] == jnp.arange(local_experts, dtype=jnp.int32)[None, None, :]
    ).astype(jnp.int32)
    local_running = jnp.cumsum(local_hot, axis=1) - local_hot
    order_all = jnp.sum(local_running * local_hot, axis=2)
    block_index = jnp.arange(blocks, dtype=jnp.int32)[:, None]
    is_mine = (local_ids >= 0) & (local_ids < local_experts)
    destination = jnp.where(
        is_mine, (local_ids * blocks + block_index) * capacity + order_all, slot_total
    )
    source_token = block_index * tok_count + token_in_block[None, :]
    slot_table = (
        jnp.full((slot_total,), blocks * tok_count, jnp.int32)
        .at[destination.reshape(-1)]
        .set(source_token.reshape(-1), mode="drop")
    )
    padded = jnp.concatenate([gathered, jnp.zeros((1, share_width), gathered.dtype)], axis=0)
    arrived = padded[slot_table].reshape(local_experts, blocks, capacity, share_width)
    slot_rows = arrived.reshape(local_experts, blocks * capacity, share_width)
    gate_terms = jnp.einsum(
        "erd,edf->erf", slot_rows, gate_up_weight[:, 0], preferred_element_type=jnp.float32
    )
    up_terms = jnp.einsum(
        "erd,edf->erf", slot_rows, gate_up_weight[:, 1], preferred_element_type=jnp.float32
    )
    gate_sum, up_sum = (
        lax.psum_scatter(
            gate_terms.astype(jnp.bfloat16), "narrow", scatter_dimension=2, tiled=True
        ).astype(jnp.float32),
        lax.psum_scatter(
            up_terms.astype(jnp.bfloat16), "narrow", scatter_dimension=2, tiled=True
        ).astype(jnp.float32),
    )
    hidden = (jax.nn.silu(gate_sum) * up_sum).astype(jnp.bfloat16)
    expert_terms = jnp.einsum(
        "erf,efd->erd", hidden, down_weight, preferred_element_type=jnp.float32
    )
    expert_out = lax.psum_scatter(
        expert_terms.astype(jnp.bfloat16), "narrow", scatter_dimension=2, tiled=True
    )
    expert_out = expert_out.reshape(local_experts, blocks, capacity, share_width)
    returned = lax.all_to_all(expert_out, "wide", split_axis=1, concat_axis=1, tiled=True)
    flat_out = returned.reshape(slot_total, share_width)
    picked = flat_out[out_index].reshape(tok_count, TOPK, share_width)
    combined = jnp.sum(weights[:, :, None] * picked.astype(jnp.float32), axis=1)
    return combined.astype(jnp.bfloat16)


def solution(mesh):
    placed = (
        P("wide", "narrow"),
        P("narrow", None),
        P("wide", None, "narrow", None),
        P("wide", "narrow", None),
        P("wide", None),
    )
    return jax.shard_map(
        local, mesh=mesh, in_specs=placed, out_specs=P("wide", "narrow"), check_vma=False
    )
```

profile of v0, /device:TPU:0, one launch (start us, length us, event | category | flops | bytes accessed | tf_op | source)
XLA Modules:
  0.0 355.1 jit_solution(15422865398020943970)
XLA Ops:
  6.5 0.7 all-gather.2.cloned.1.call-update
  7.3 0.7 convert_element_type.56
  8.0 27.9 %all_gather.7 = bf16[1024,8]{0,1:T(8,128)(2,1)S(1)} all-gather(bf16[128,8]{0,1:T(8,128)(2,1)S(1)} %convert_element_type.56), channel_id=1, replica_groups=mesh['narrow'=4,'wide'=8] {'wide'}, dimensions={0}, use_global_device_ids=true | all-gather | bytes 18432 | tf_op jit(solution)/shard_map/all_gather | solution.py:39
  36.2 0.3 sub.55
  36.4 0.3 sub.54
  36.8 36.0 %reduce-window.14 = s32[8,16,8,128]{3,2,1,0:T(8,128)S(1)} reduce-window(s32[8,16,8,128]{3,2,1,0:T(8,128)S(1)} %fusion.26, s32[]{:T(128)} %constant.58.clone.1), window={size=1x1x1x128 pad=0_0x0_0x0_0x127_0}, to_apply=%region_3.0 | reduce-window | flops 16646144 | bytes 1048580 | tf_op jit(solution)/shard_map/reduce-window
  72.8 0.2 slice.28
  73.0 0.5 copy.42
  73.6 0.2 broadcast_add_fusion.1
  74.3 0.3 mul.105
  74.6 0.3 copy.38
  74.9 0.3 and.47
  75.4 30.4 %scatter_custom_fusion = s32[2048]{0:T(1024)S(1)} fusion(s32[8192]{0:T(1024)S(1)} %bitcast.67, s32[8192]{0:T(1024)S(1)} %bitcast.68, s32[]{:T(128)} %constant.55.clone.1), kind=kCustom, calls=%fused_computation.64 | custom fusion | bytes 8196 | tf_op jit(solution)/shard_map/scatter | solution.py:58
  105.9 1.3 concatenate.3
  107.2 7.5 %gather_fusion = bf16[2048,512]{1,0:T(8,128)(2,1)S(1)} fusion(bf16[1025,512]{1,0:T(8,128)(2,1)S(1)} %concatenate.3, s32[2048]{0:T(1024)S(1)} %fusion.28), kind=kCustom, calls=%fused_computation | custom fusion | bytes 4202496 | tf_op jit(solution)/shard_map/gather | solution.py:61
  114.7 9.9 %fusion.6 = bf16[16,128,768]{1,2,0:T(8,128)(2,1)} fusion(bf16[16,128,512]{2,1,0:T(8,128)(2,1)S(1)} %bitcast.60, bf16[16,2,512,768]{3,2,1,0:T(8,128)(2,1)} %param.7), kind=kOutput, calls=%fused_computation.10 | convolution fusion | flops 1612185600 | bytes 17825792 | tf_op jit(solution)/shard_map/erd,edf->erf/dot_general | solution.py:63
  124.7 0.2 reduce-scatter.6.cloned.1.call-start
  124.9 10.0 %fusion.9 = bf16[16,128,768]{1,2,0:T(8,128)(2,1)} fusion(bf16[16,128,512]{2,1,0:T(8,128)(2,1)S(1)} %bitcast.61, bf16[16,2,512,768]{3,2,1,0:T(8,128)(2,1)} %param.7), kind=kOutput, calls=%fused_computation.11 | convolution fusion | flops 1612185600 | bytes 17825792 | tf_op jit(solution)/shard_map/erd,edf->erf/dot_general | solution.py:66
  134.9 27.1 %reduce-scatter.4.cloned.1.call-done = bf16[16,128,192]{1,2,0:T(8,128)(2,1)} async-done(((bf16[16,128,768]{1,2,0:T(8,128)(2,1)}), bf16[16,128,192]{1,2,0:T(8,128)(2,1)}) %reduce-scatter.4.cloned.1.call-update) | async-done | bytes 786448 | tf_op jit(solution)/shard_map/reduce_scatter | solution.py:70
  162.0 40.3 %reduce-scatter.6.cloned.1.call-done = bf16[16,128,192]{1,2,0:T(8,128)(2,1)} async-done(((bf16[16,128,768]{1,2,0:T(8,128)(2,1)}), bf16[16,128,192]{1,2,0:T(8,128)(2,1)}) %reduce-scatter.6.cloned.1.call-update) | async-done | bytes 786448 | tf_op jit(solution)/shard_map/reduce_scatter | solution.py:73
  202.4 10.7 %convolution_convert_fusion = bf16[16,128,2048]{2,1,0:T(8,128)(2,1)} fusion(bf16[16,192,2048]{2,1,0:T(8,128)(2,1)} %param.8, bf16[16,128,192]{1,2,0:T(8,128)(2,1)} %reduce-scatter.6.cloned.1.call-done, bf16[16,128,192]{1,2,0:T(8,128)(2,1)} %reduce-scatter.4.cloned.1.call-done), kind=kOutput, calls=%fused_computation.9 | convolution fusion | flops 1617952768 | bytes 22544384 | tf_op jit(solution)/shard_map/erf,efd->erd/dot_general | solution.py:78
  213.1 71.4 %reduce-scatter.8.cloned.1.call-done = bf16[16,128,512]{2,1,0:T(8,128)(2,1)} async-done(((bf16[16,128,2048]{2,1,0:T(8,128)(2,1)}), bf16[16,128,512]{2,1,0:T(8,128)(2,1)}) %reduce-scatter.8.cloned.1.call-update) | async-done | bytes 2097168 | tf_op jit(solution)/shard_map/reduce_scatter | solution.py:81
  284.5 3.2 copy.46
  287.6 5.6 %all-to-all-start = ((bf16[16,8,16,512]{3,2,0,1:T(8,128)(2,1)}), bf16[16,8,16,512]{3,2,0,1:T(8,128)(2,1)}, u32[]{:S(2)}, u32[]{:S(2)}) async-start(bf16[16,8,16,512]{3,2,0,1:T(8,128)(2,1)} %copy.46), calls=%async_computation.3 | async-start | bytes 4194304 | tf_op jit(solution)/shard_map/all_to_all | solution.py:85
  293.8 0.2 fusion.24
  294.4 11.1 %psum.7 = bf16[128,128]{1,0:T(8,128)(2,1)S(1)} all-reduce(bf16[128,128]{1,0:T(8,128)(2,1)S(1)} %convolution_convert_fusion.1), channel_id=1, replica_groups=mesh['narrow'=4,'wide'=8] {'narrow'}, use_global_device_ids=true, to_apply=%region_0.0 | all-reduce | flops 16384 | bytes 65536 | tf_op jit(solution)/shard_map/psum | solution.py:18
  305.5 0.4 select_reduce_fusion
  306.0 0.4 fusion.21
  306.5 35.0 %all-to-all-done = bf16[16,8,16,512]{3,2,0,1:T(8,128)(2,1)} async-done(((bf16[16,8,16,512]{3,2,0,1:T(8,128)(2,1)}), bf16[16,8,16,512]{3,2,0,1:T(8,128)(2,1)}, u32[]{:S(2)}, u32[]{:S(2)}) %all-to-all-start) | async-done | bytes 2097184 | tf_op jit(solution)/shard_map/all_to_all | solution.py:85
  341.5 1.8 copy.47
  343.2 4.0 %gather_fusion.1 = bf16[1024,512]{1,0:T(8,128)(2,1)S(1)} fusion(bf16[2048,512]{1,0:T(8,128)(2,1)S(1)} %bitcast.59, s32[1024]{0:T(1024)S(1)} %broadcast_clamp_fusion), kind=kCustom, calls=%fused_computation.1 | custom fusion | bytes 2101248 | tf_op jit(solution)/shard_map/gather | solution.py:87
  347.2 1.4 fusion.12
  (48 shorter events, 2.3 us)
Async XLA Ops:
  6.5 287.7 %copy-start = (bf16[512,128]{1,0:T(8,128)(2,1)S(1)}, bf16[512,128]{1,0:T(8,128)(2,1)}, u32[]{:S(2)}) copy-start(bf16[512,128]{1,0:T(8,128)(2,1)} %param.6) | copy-start | bytes 393220
  6.5 99.3 %all-gather.2.cloned.1.call-start = ((), (), s32[]{:S(2)}) async-start(), calls=%async_computation.4 | async-start | bytes 1179648 | tf_op jit(solution)/shard_map/all_gather | solution.py:38
  7.3 154.8 %reduce-scatter.4.cloned.1.call-start = ((), (), s32[]{:S(2)}) async-start(), calls=%async_computation.5 | async-start | bytes 3932160 | tf_op jit(solution)/shard_map/reduce_scatter | solution.py:70
  124.7 77.7 %reduce-scatter.6.cloned.1.call-start = ((), (), s32[]{:S(2)}) async-start(), calls=%async_computation.6 | async-start | bytes 3932160 | tf_op jit(solution)/shard_map/reduce_scatter | solution.py:73
  134.9 149.6 %reduce-scatter.8.cloned.1.call-start = ((), (), s32[]{:S(2)}) async-start(), calls=%async_computation.7 | async-start | bytes 10485760 | tf_op jit(solution)/shard_map/reduce_scatter | solution.py:81
  287.6 5.6 %copy-start.2 = (s32[128,8]{0,1:T(8,128)S(1)}, s32[128,8]{0,1:T(8,128)}, u32[]{:S(2)}) copy-start(s32[128,8]{0,1:T(8,128)} %param.9) | copy-start | bytes 12292
  287.6 53.8 %all-to-all-start = ((bf16[16,8,16,512]{3,2,0,1:T(8,128)(2,1)}), bf16[16,8,16,512]{3,2,0,1:T(8,128)(2,1)}, u32[]{:S(2)}, u32[]{:S(2)}) async-start(bf16[16,8,16,512]{3,2,0,1:T(8,128)(2,1)} %copy.46), calls=%async_computation.3 | async-start | bytes 4194304 | tf_op jit(solution)/shard_map/all_to_all | solution.py:85
  293.3 0.9 copy-start.1
Sparse Core Ops, SparseCore 0:
  9.5 42.9 all-gather.1
  124.8 37.1 reduce-scatter.3
  164.6 37.7 reduce-scatter.5
  213.2 71.2 reduce-scatter.7
where the time goes:
time: 356 us; the launch traced here: 355 us
  waiting for transfers between devices  175 us (49%)
  local copies, waits for them, and re-layouts  51.5 us (14%)
  other arithmetic  40 us (11%)
  blocking collectives  39 us (11%)
  matrix products  30.7 us (9%)
  between operations  13.4 us (4%)
  starting transfers between devices  5.94 us (2%)
    reduce_scatter x1, waiting for transfers between devices, local(): lax.psum_scatter(expert_terms.astype(jnp.bfloat16), 'narrow', scatter_dim...  71.4 us
    reduce_scatter x1, waiting for transfers between devices, local(): lax.psum_scatter(up_terms.astype(jnp.bfloat16), 'narrow', scatter_dimensi...  40.3 us
    another operation x6, other arithmetic  36.5 us
    all_to_all x1, waiting for transfers between devices, local(): lax.all_to_all(expert_out, 'wide', split_axis=1, concat_axis=1, tiled=True)  35 us
    scatter x1, local copies, waits for them, and re-layouts, local(): slot_table = jnp.full((slot_total,), blocks * tok_count, jnp.int32).at[de...  30.4 us
    all_gather x1, blocking collectives, local(): lax.all_gather(expert_ids.astype(jnp.bfloat16), 'wide', axis=0, tiled=True)  27.9 us
    reduce_scatter x1, waiting for transfers between devices, local(): lax.psum_scatter(gate_terms.astype(jnp.bfloat16), 'narrow', scatter_dimen...  27.1 us
    psum x1, blocking collectives, local(): lax.psum(jnp.dot(normed, router_weight, preferred_element_type=jnp.float3...  11.1 us
  transfers between devices with their start and end apart: 5, of which 4 were waited for; matrix products, arithmetic and copies ran while one was open for 23% of the time, Pallas kernels for 0%

commit v1 on v0

--- a/solution.py
+++ b/solution.py
@@ -5,6 +5,28 @@
 
 TOPK = 8
 CAP = 16
+
+
+def test_samples_all(array_in, k_dim, dimension_no):
+    y1, value_now = (lax.axis_size("wide"), lax.axis_index("wide"))
+    outcome_arr = array_in.shape[k_dim] // y1
+    mat_out = list(array_in.shape)
+    mat_out[k_dim] = outcome_arr
+    mid_arr = mat_out[dimension_no]
+    mat_out[dimension_no] = mid_arr * y1
+    small = jnp.zeros(mat_out, array_in.dtype)
+    m = 0
+    while m < y1:
+        block_out = lax.dynamic_slice_in_dim(
+            array_in, (value_now ^ m) * outcome_arr, outcome_arr, axis=k_dim
+        )
+        if m:
+            block_out = lax.ppermute(block_out, "wide", [(u, u ^ m) for u in range(y1)])
+        small = lax.dynamic_update_slice_in_dim(
+            small, block_out, (value_now ^ m) * mid_arr, axis=dimension_no
+        )
+        m += 1
+    return small
 
 
 def local(normed, router_weight, gate_up_weight, down_weight, expert_ids):
@@ -82,7 +104,7 @@
         expert_terms.astype(jnp.bfloat16), "narrow", scatter_dimension=2, tiled=True
     )
     expert_out = expert_out.reshape(local_experts, blocks, capacity, share_width)
-    returned = lax.all_to_all(expert_out, "wide", split_axis=1, concat_axis=1, tiled=True)
+    returned = test_samples_all(expert_out, 1, 1)
     flat_out = returned.reshape(slot_total, share_width)
     picked = flat_out[out_index].reshape(tok_count, TOPK, share_width)
     combined = jnp.sum(weights[:, :, None] * picked.astype(jnp.float32), axis=1)

time: 356 us -> 349 us (0.980)
  the two profiles are of different devices: /device:TPU:0 before, /device:TPU:16 now
where the time goes in v1:
time: 349 us; the launch traced here: 348 us
  waiting for transfers between devices  172 us (49%)
  local copies, waits for them, and re-layouts  49.1 us (14%)
  other arithmetic  39.9 us (11%)
  blocking collectives  34.2 us (10%)
  matrix products  30.7 us (9%)
  between operations  13.6 us (4%)
  starting transfers between devices  8.51 us (2%)
    reduce_scatter x1, waiting for transfers between devices, local(): lax.psum_scatter(expert_terms.astype(jnp.bfloat16), 'narrow', scatter_dim...  58.2 us
    ppermute x7, waiting for transfers between devices, test_samples_all(): block_out = lax.ppermute(block_out, 'wide', [(u, u ^ m) for u in range(y1)])  43.5 us
    reduce_scatter x1, waiting for transfers between devices, local(): lax.psum_scatter(up_terms.astype(jnp.bfloat16), 'narrow', scatter_dimensi...  40.3 us
    another operation x6, other arithmetic  36.5 us
    scatter x1, local copies, waits for them, and re-layouts, local(): slot_table = jnp.full((slot_total,), blocks * tok_count, jnp.int32).at[de...  30.4 us
    reduce_scatter x1, waiting for transfers between devices, local(): lax.psum_scatter(gate_terms.astype(jnp.bfloat16), 'narrow', scatter_dimen...  29.5 us
    all_gather x1, blocking collectives, local(): lax.all_gather(expert_ids.astype(jnp.bfloat16), 'wide', axis=0, tiled=True)  23.8 us
    dot_general x1, matrix products, local(): jnp.einsum('erf,efd->erd', hidden, down_weight, preferred_element_type=jn...  10.7 us
  transfers between devices with their start and end apart: 11, of which 9 were waited for; matrix products, arithmetic and copies ran while one was open for 24% of the time, Pallas kernels for 0%

profile of v1, /device:TPU:16, one launch (start us, length us, event | category | flops | bytes accessed | tf_op | source)
XLA Modules:
  0.0 348.4 jit_solution(1657535062200965172)
XLA Ops:
  6.5 0.7 all-gather.2.cloned.1.call-update
  7.3 0.7 convert_element_type.56
  8.0 23.8 %all_gather.7 = bf16[1024,8]{0,1:T(8,128)(2,1)S(1)} all-gather(bf16[128,8]{0,1:T(8,128)(2,1)S(1)} %convert_element_type.56), channel_id=1, replica_groups=mesh['narrow'=4,'wide'=8] {'wide'}, dimensions={0}, use_global_device_ids=true | all-gather | bytes 18432 | tf_op jit(solution)/shard_map/all_gather | solution.py:61
  32.7 36.0 %reduce-window.14 = s32[8,16,8,128]{3,2,1,0:T(8,128)S(1)} reduce-window(s32[8,16,8,128]{3,2,1,0:T(8,128)S(1)} %fusion.26, s32[]{:T(128)} %constant.35.clone.1), window={size=1x1x1x128 pad=0_0x0_0x0_0x127_0}, to_apply=%region_3.0 | reduce-window | flops 16646144 | bytes 1048580 | tf_op jit(solution)/shard_map/reduce-window
  68.9 0.5 copy.26
  71.3 30.4 %scatter_custom_fusion = s32[2048]{0:T(1024)S(1)} fusion(s32[8192]{0:T(1024)S(1)} %bitcast.67, s32[8192]{0:T(1024)S(1)} %bitcast.68, s32[]{:T(128)} %constant.29.clone.1), kind=kCustom, calls=%fused_computation.79 | custom fusion | bytes 8196 | tf_op jit(solution)/shard_map/scatter | solution.py:80
  101.8 1.3 concatenate.3
  103.1 7.5 %gather_fusion = bf16[2048,512]{1,0:T(8,128)(2,1)S(1)} fusion(bf16[1025,512]{1,0:T(8,128)(2,1)S(1)} %concatenate.3, s32[2048]{0:T(1024)S(1)} %fusion.28), kind=kCustom, calls=%fused_computation | custom fusion | bytes 4202496 | tf_op jit(solution)/shard_map/gather | solution.py:83
  110.6 9.9 %fusion.6 = bf16[16,128,768]{1,2,0:T(8,128)(2,1)} fusion(bf16[16,128,512]{2,1,0:T(8,128)(2,1)S(1)} %bitcast.60, bf16[16,2,512,768]{3,2,1,0:T(8,128)(2,1)} %param.7), kind=kOutput, calls=%fused_computation.10 | convolution fusion | flops 1612185600 | bytes 17825792 | tf_op jit(solution)/shard_map/erd,edf->erf/dot_general | solution.py:85
  120.8 10.0 %fusion.9 = bf16[16,128,768]{1,2,0:T(8,128)(2,1)} fusion(bf16[16,128,512]{2,1,0:T(8,128)(2,1)S(1)} %bitcast.61, bf16[16,2,512,768]{3,2,1,0:T(8,128)(2,1)} %param.7), kind=kOutput, calls=%fused_computation.11 | convolution fusion | flops 1612185600 | bytes 17825792 | tf_op jit(solution)/shard_map/erd,edf->erf/dot_general | solution.py:88
  130.8 29.5 %reduce-scatter.4.cloned.1.call-done = bf16[16,128,192]{1,2,0:T(8,128)(2,1)} async-done(((bf16[16,128,768]{1,2,0:T(8,128)(2,1)}), bf16[16,128,192]{1,2,0:T(8,128)(2,1)}) %reduce-scatter.4.cloned.1.call-update) | async-done | bytes 786448 | tf_op jit(solution)/shard_map/reduce_scatter | solution.py:92
  160.4 40.3 %reduce-scatter.6.cloned.1.call-done = bf16[16,128,192]{1,2,0:T(8,128)(2,1)} async-done(((bf16[16,128,768]{1,2,0:T(8,128)(2,1)}), bf16[16,128,192]{1,2,0:T(8,128)(2,1)}) %reduce-scatter.6.cloned.1.call-update) | async-done | bytes 786448 | tf_op jit(solution)/shard_map/reduce_scatter | solution.py:95
  200.7 10.7 %convolution_convert_fusion = bf16[16,128,2048]{2,1,0:T(8,128)(2,1)} fusion(bf16[16,192,2048]{2,1,0:T(8,128)(2,1)} %param.8, bf16[16,128,192]{1,2,0:T(8,128)(2,1)} %reduce-scatter.6.cloned.1.call-done, bf16[16,128,192]{1,2,0:T(8,128)(2,1)} %reduce-scatter.4.cloned.1.call-done), kind=kOutput, calls=%fused_computation.9 | convolution fusion | flops 1617952768 | bytes 22544384 | tf_op jit(solution)/shard_map/erf,efd->erd/dot_general | solution.py:100
  211.5 0.6 copy-done.3
  213.2 10.4 %psum.7 = bf16[128,128]{1,0:T(8,128)(2,1)S(1)} all-reduce(bf16[128,128]{1,0:T(8,128)(2,1)S(1)} %convolution_convert_fusion.1), channel_id=1, replica_groups=mesh['narrow'=4,'wide'=8] {'narrow'}, use_global_device_ids=true, to_apply=%region_0.0 | all-reduce | flops 16384 | bytes 65536 | tf_op jit(solution)/shard_map/psum | solution.py:40
  224.1 0.4 fusion.21
  224.6 58.2 %reduce-scatter.8.cloned.1.call-done = bf16[16,128,512]{2,1,0:T(8,128)(2,1)} async-done(((bf16[16,128,2048]{2,1,0:T(8,128)(2,1)}), bf16[16,128,512]{2,1,0:T(8,128)(2,1)}) %reduce-scatter.8.cloned.1.call-update) | async-done | bytes 2097168 | tf_op jit(solution)/shard_map/reduce_scatter | solution.py:103
  283.1 1.3 copy-done.1
  284.7 1.5 collective-permute-start
  286.2 1.5 collective-permute-start.1
  287.8 0.6 collective-permute-start.2
  288.3 0.5 collective-permute-start.3
  288.8 3.3 collective-permute-start.4
  292.2 0.7 collective-permute-done
  292.9 0.5 collective-permute-start.5
  293.5 9.9 %collective-permute-done.1 = bf16[16,1,16,512]{3,2,1,0:T(8,128)(2,1)S(1)} collective-permute-done((bf16[16,1,16,512]{3,2,1,0:T(8,128)(2,1)S(1)}, bf16[16,1,16,512]{3,2,1,0:T(8,128)(2,1)S(1)}, u32[]{:S(2)}, u32[]{:S(2)}) %collective-permute-start.1) | collective-permute-done | bytes 262176 | tf_op jit(solution)/shard_map/ppermute | solution.py:24
  303.6 3.8 %collective-permute-done.2 = bf16[16,1,16,512]{3,2,1,0:T(8,128)(2,1)S(1)} collective-permute-done((bf16[16,1,16,512]{3,2,1,0:T(8,128)(2,1)S(1)}, bf16[16,1,16,512]{3,2,1,0:T(8,128)(2,1)S(1)}, u32[]{:S(2)}, u32[]{:S(2)}) %collective-permute-start.2) | collective-permute-done | bytes 262176 | tf_op jit(solution)/shard_map/ppermute | solution.py:24
  307.5 16.2 %collective-permute-done.4 = bf16[16,1,16,512]{3,2,1,0:T(8,128)(2,1)S(1)} collective-permute-done((bf16[16,1,16,512]{3,2,1,0:T(8,128)(2,1)S(1)}, bf16[16,1,16,512]{3,2,1,0:T(8,128)(2,1)S(1)}, u32[]{:S(2)}, u32[]{:S(2)}) %collective-permute-start.4) | collective-permute-done | bytes 262176 | tf_op jit(solution)/shard_map/ppermute | solution.py:24
  323.6 8.5 %collective-permute-done.5 = bf16[16,1,16,512]{3,2,1,0:T(8,128)(2,1)S(1)} collective-permute-done((bf16[16,1,16,512]{3,2,1,0:T(8,128)(2,1)S(1)}, bf16[16,1,16,512]{3,2,1,0:T(8,128)(2,1)S(1)}, u32[]{:S(2)}, u32[]{:S(2)}) %collective-permute-start.5) | collective-permute-done | bytes 262176 | tf_op jit(solution)/shard_map/ppermute | solution.py:24
  332.2 4.4 %collective-permute-done.6 = bf16[16,1,16,512]{3,2,1,0:T(8,128)(2,1)S(1)} collective-permute-done((bf16[16,1,16,512]{3,2,1,0:T(8,128)(2,1)S(1)}, bf16[16,1,16,512]{3,2,1,0:T(8,128)(2,1)S(1)}, u32[]{:S(2)}, u32[]{:S(2)}) %collective-permute-start.6) | collective-permute-done | bytes 262176 | tf_op jit(solution)/shard_map/ppermute | solution.py:24
  336.6 4.0 %gather_fusion.1 = bf16[1024,512]{1,0:T(8,128)(2,1)S(1)} fusion(bf16[2048,512]{1,0:T(8,128)(2,1)S(1)} %bitcast.59, s32[1024]{0:T(1024)S(1)} %broadcast_clamp_fusion), kind=kCustom, calls=%fused_computation.1 | custom fusion | bytes 2101248 | tf_op jit(solution)/shard_map/gather | solution.py:109
  340.6 1.3 fusion.12
  (69 shorter events, 5.7 us)
Async XLA Ops:
  6.5 206.5 %copy-start = (bf16[512,128]{1,0:T(8,128)(2,1)S(1)}, bf16[512,128]{1,0:T(8,128)(2,1)}, u32[]{:S(2)}) copy-start(bf16[512,128]{1,0:T(8,128)(2,1)} %param.6) | copy-start | bytes 393220
  6.5 95.2 %all-gather.2.cloned.1.call-start = ((), (), s32[]{:S(2)}) async-start(), calls=%async_computation.3 | async-start | bytes 1179648 | tf_op jit(solution)/shard_map/all_gather | solution.py:60
  7.3 153.1 %reduce-scatter.4.cloned.1.call-start = ((), (), s32[]{:S(2)}) async-start(), calls=%async_computation.4 | async-start | bytes 3932160 | tf_op jit(solution)/shard_map/reduce_scatter | solution.py:92
  120.6 80.2 %reduce-scatter.6.cloned.1.call-start = ((), (), s32[]{:S(2)}) async-start(), calls=%async_computation.5 | async-start | bytes 3932160 | tf_op jit(solution)/shard_map/reduce_scatter | solution.py:95
  130.8 152.1 %reduce-scatter.8.cloned.1.call-start = ((), (), s32[]{:S(2)}) async-start(), calls=%async_computation.6 | async-start | bytes 10485760 | tf_op jit(solution)/shard_map/reduce_scatter | solution.py:103
  211.4 0.7 copy-start.3
  211.4 1.6 copy-start.2
  282.8 1.6 copy-start.1
  284.7 8.2 %collective-permute-start = (bf16[16,1,16,512]{3,2,1,0:T(8,128)(2,1)S(1)}, bf16[16,1,16,512]{3,2,1,0:T(8,128)(2,1)S(1)}, u32[]{:S(2)}, u32[]{:S(2)}) collective-permute-start(bf16[16,1,16,512]{3,2,1,0:T(8,128)(2,1)S(1)} %get-tuple-element.11), channel_id=1, source_target_pairs={{0,1},{1,0},{2,3},{3,2},{4,5},{5,4},{6,7},{7,6},{8,9},{9,8},{10,11... | collective-permute-start | bytes 786440 | tf_op jit(solution)/shard_map/ppermute | solution.py:24
  286.2 17.1 %collective-permute-start.1 = (bf16[16,1,16,512]{3,2,1,0:T(8,128)(2,1)S(1)}, bf16[16,1,16,512]{3,2,1,0:T(8,128)(2,1)S(1)}, u32[]{:S(2)}, u32[]{:S(2)}) collective-permute-start(bf16[16,1,16,512]{3,2,1,0:T(8,128)(2,1)S(1)} %get-tuple-element.10), channel_id=1, source_target_pairs={{0,2},{1,3},{2,0},{3,1},{4,6},{5,7},{6,4},{7,5},{8,10},{9,11},{10,... | collective-permute-start | bytes 786440 | tf_op jit(solution)/shard_map/ppermute | solution.py:24
  287.8 19.6 %collective-permute-start.2 = (bf16[16,1,16,512]{3,2,1,0:T(8,128)(2,1)S(1)}, bf16[16,1,16,512]{3,2,1,0:T(8,128)(2,1)S(1)}, u32[]{:S(2)}, u32[]{:S(2)}) collective-permute-start(bf16[16,1,16,512]{3,2,1,0:T(8,128)(2,1)S(1)} %get-tuple-element.9), channel_id=1, source_target_pairs={{0,3},{1,2},{2,1},{3,0},{4,7},{5,6},{6,5},{7,4},{8,11},{9,10},{10,... | collective-permute-start | bytes 786440 | tf_op jit(solution)/shard_map/ppermute | solution.py:24
  288.3 19.1 %collective-permute-start.3 = (bf16[16,1,16,512]{3,2,1,0:T(8,128)(2,1)S(1)}, bf16[16,1,16,512]{3,2,1,0:T(8,128)(2,1)S(1)}, u32[]{:S(2)}, u32[]{:S(2)}) collective-permute-start(bf16[16,1,16,512]{3,2,1,0:T(8,128)(2,1)S(1)} %get-tuple-element.8), channel_id=1, source_target_pairs={{0,4},{1,5},{2,6},{3,7},{4,0},{5,1},{6,2},{7,3},{8,12},{9,13},{10,... | collective-permute-start | bytes 786440 | tf_op jit(solution)/shard_map/ppermute | solution.py:24
  288.8 34.8 %collective-permute-start.4 = (bf16[16,1,16,512]{3,2,1,0:T(8,128)(2,1)S(1)}, bf16[16,1,16,512]{3,2,1,0:T(8,128)(2,1)S(1)}, u32[]{:S(2)}, u32[]{:S(2)}) collective-permute-start(bf16[16,1,16,512]{3,2,1,0:T(8,128)(2,1)S(1)} %get-tuple-element.7), channel_id=1, source_target_pairs={{0,5},{1,4},{2,7},{3,6},{4,1},{5,0},{6,3},{7,2},{8,13},{9,12},{10,... | collective-permute-start | bytes 786440 | tf_op jit(solution)/shard_map/ppermute | solution.py:24
  292.9 39.2 %collective-permute-start.5 = (bf16[16,1,16,512]{3,2,1,0:T(8,128)(2,1)S(1)}, bf16[16,1,16,512]{3,2,1,0:T(8,128)(2,1)S(1)}, u32[]{:S(2)}, u32[]{:S(2)}) collective-permute-start(bf16[16,1,16,512]{3,2,1,0:T(8,128)(2,1)S(1)} %get-tuple-element.6), channel_id=1, source_target_pairs={{0,6},{1,7},{2,4},{3,5},{4,2},{5,3},{6,0},{7,1},{8,14},{9,15},{10,... | collective-permute-start | bytes 786440 | tf_op jit(solution)/shard_map/ppermute | solution.py:24
  303.3 33.2 %collective-permute-start.6 = (bf16[16,1,16,512]{3,2,1,0:T(8,128)(2,1)S(1)}, bf16[16,1,16,512]{3,2,1,0:T(8,128)(2,1)S(1)}, u32[]{:S(2)}, u32[]{:S(2)}) collective-permute-start(bf16[16,1,16,512]{3,2,1,0:T(8,128)(2,1)S(1)} %get-tuple-element.5), channel_id=1, source_target_pairs={{0,7},{1,6},{2,5},{3,4},{4,3},{5,2},{6,1},{7,0},{8,15},{9,14},{10,... | collective-permute-start | bytes 786440 | tf_op jit(solution)/shard_map/ppermute | solution.py:24
Sparse Core Ops, SparseCore 0:
  9.5 39.5 all-gather.1
  120.7 39.6 reduce-scatter.3
  162.9 37.7 reduce-scatter.5
  211.6 71.2 reduce-scatter.7
